TPU v7x, 32 devices: a whole 2x2x4 slice. The times are simulated.
32 devices in a mesh: groups: 2 (over x), row: 8 (over z, y), col: 2 (over core).
Axes of the slice: x: 2, y: 2, z: 4, core: 2. Of those that a mesh axis runs over, the one named last changes fastest.
Arguments:
- pair_rep: bfloat16 [160, 80, 128], P(('groups', 'row'), 'col'), parts along dimension 0, as said below
- proj_weight: bfloat16 [128, 512], replicated, may hold values from -0.5 to 0.5
- gate_weight: bfloat16 [128, 128], replicated, may hold values from -0.5 to 0.5
- out_weight: bfloat16 [128, 128], replicated, may hold values from -0.5 to 0.5
Outputs:
- update: bfloat16 [160, 80, 128], P(('groups', 'row'), 'col'), parts along dimension 0
There are 2 independent parts, one for each index of `groups`. A program takes and returns all parts, laid end to end along the dimension named above; an argument that names none is the same for every part. Nothing has to cross between parts.
Inputs may be any that keep to these rules, and one draw needn't show every extreme that they name: `pair_rep`: real-valued pair features; each pair position and each channel carries its own scale factor between 1 and 10.
All inputs are finite; a program needn't handle non-finite values.
Results may differ from a plain program's by a relative error of at most 0.0078.
Values may be sent and summed in bfloat16 or wider, within the bound.
A program may use at most 128 MiB of HBM per device.

v0:
```python
import functools

import jax
import jax.numpy as jnp
from jax import lax
from jax.experimental import pallas as pl
from jax.experimental.pallas import tpu as pltpu
from jax.sharding import PartitionSpec as P

MESH = pl.DeviceIdType.MESH
F32 = jnp.float32
BF16 = jnp.bfloat16


def layer_norm(values):
    average = jnp.mean(values, axis=-1, keepdims=True)
    centered = values - average
    spread = jnp.mean(centered * centered, axis=-1, keepdims=True)
    return centered * lax.rsqrt(spread + 1e-05)


def kernel(
    n, rows, cols, pairs, sub, x_hbm, wp_hbm, wg_hbm, wo_hbm, out_ref,
    x_ref, wp_ref, wg_ref, wo_ref, normed, in_sem, own, right, left, left32, comb, gate, stage, back,
    own_send, fwd_send, recv, lsend, lrecv, ret_send, ret_recv,
):
    hid = wo_ref.shape[0]
    chunks = pairs * sub
    flat = rows * cols
    part = flat // pairs
    loads = [pltpu.make_async_copy(x_hbm, x_ref, in_sem.at[0])]
    for k in (1, 0):
        cut = (slice(None), pl.ds(2 * hid * k, 2 * hid))
        loads.append(pltpu.make_async_copy(wp_hbm.at[cut], wp_ref.at[k], in_sem.at[len(loads)]))
    loads.append(pltpu.make_async_copy(wg_hbm, wg_ref, in_sem.at[3]))
    loads.append(pltpu.make_async_copy(wo_hbm, wo_ref, in_sem.at[4]))
    for load in loads:
        load.start()
    deep = n // 2
    span = deep // 2
    row, c = lax.axis_index("row"), lax.axis_index("col")
    z, y = row // 2, row % 2
    across = 2 * z + 1 - y
    has_up, has_down = z < deep - 1, z > 0
    low = c * span
    barrier = pltpu.get_barrier_semaphore()

    def greet(r, cc):
        pl.semaphore_signal(barrier, inc=1, device_id={"row": r, "col": cc}, device_id_type=MESH)

    greet(row, 1 - c)
    greet(across, c)

    @pl.when(has_up)
    def _():
        for cc in range(2):
            greet(row + 2, cc)

    @pl.when(has_down)
    def _():
        for cc in range(2):
            greet(row - 2, cc)

    dest = z // span
    my_slot = z - dest * span
    step = flat // chunks

    def gated(values, k):
        proj = jnp.dot(values, wp_ref[k], preferred_element_type=F32)
        return (jax.nn.sigmoid(proj[:, :hid]) * proj[:, hid:]).astype(BF16)

    def prepare(p):
        here = pl.ds(p * part, part)
        values = layer_norm(x_ref[here, :].astype(F32)).astype(BF16)
        normed[here, :] = values
        own[here, :] = gated(values, 1)

    loads[0].wait()
    loads[1].wait()

    def own_copy(way, q, r):
        return pltpu.make_async_remote_copy(
            src_ref=own.at[pl.ds(q * step, step)],
            dst_ref=right.at[my_slot, c, pl.ds(q * step, step)],
            send_sem=own_send.at[way, q],
            recv_sem=recv.at[my_slot, c, q],
            device_id={"row": r, "col": dest},
            device_id_type=MESH,
        )

    ways = ((0, has_down, row - 2), (1, has_up, row + 2), (2, dest != c, row))

    def own_all(p, act):
        for way, cond, r in ways:
            @pl.when(cond)
            def _(way=way, r=r):
                for q in range(p * sub, (p + 1) * sub):
                    act(own_copy(way, q, r))

    prepare(0)
    greeted = 2 + 2 * has_up.astype(jnp.int32) + 2 * has_down.astype(jnp.int32)
    pl.semaphore_wait(barrier, greeted)
    for p in range(1, pairs):
        prepare(p)
        own_all(p - 1, lambda copy: copy.start())
    own_all(pairs - 1, lambda copy: copy.start())

    @pl.when(dest == c)
    def _():
        right[my_slot, c] = own[...]

    def left_copy(which, kc, way, r, cc):
        part = left.at[which, kc]
        return pltpu.make_async_remote_copy(
            src_ref=part, dst_ref=part, send_sem=lsend.at[way], recv_sem=lrecv.at[which, kc],
            device_id={"row": r, "col": cc}, device_id_type=MESH,
        )

    loads[2].wait()
    loads[3].wait()
    mine = gated(normed[...], 0)
    left[y, c] = mine
    left32[y, c] = mine.astype(F32)
    gate[...] = jax.nn.sigmoid(jnp.dot(normed[...], wg_ref[...], preferred_element_type=F32))
    left_copy(y, c, 0, across, c).start()
    left_copy(y, c, 1, row, 1 - c).start()

    def source(t):
        inside = low + lax.rem(z - low + t + 1 + deep, span)
        return jnp.where(z < low, low + t, jnp.where(z >= low + span, low + span - 1 - t, inside))

    def passes(zs):
        return ((zs < z) & has_up) | ((zs > z) & has_down)

    def block(slot, kc, q, r):
        part = right.at[slot, kc, pl.ds(q * step, step)]
        return pltpu.make_async_remote_copy(
            src_ref=part, dst_ref=part, send_sem=fwd_send.at[slot, kc, q],
            recv_sem=recv.at[slot, kc, q], device_id={"row": r, "col": c}, device_id_type=MESH,
        )

    def send_on(t, q):
        zs = source(t)

        @pl.when(passes(zs))
        def _():
            for kc in range(2):
                block(zs - low, kc, q, row).wait_recv()
                block(zs - low, kc, q, jnp.where(zs < z, row + 2, row - 2)).start()

    early = chunks - 2 * sub
    pl.loop(0, early)(lambda q: send_on(0, q))
    left_copy(1 - y, c, 2, row, 1 - c).wait_recv()
    left_copy(1 - y, c, 2, row, 1 - c).start()
    pl.loop(early, chunks)(lambda q: send_on(0, q))

    @pl.loop(1, span)
    def _(t):
        pl.loop(0, chunks)(lambda q: send_on(t, q))

    left32[1 - y, c] = left[1 - y, c].astype(F32)
    for which in (y, 1 - y):
        left_copy(which, 1 - c, 0, row, c).wait_recv()
        left32[which, 1 - c] = left[which, 1 - c].astype(F32)

    def ret_copy(slot, pair):
        return pltpu.make_async_remote_copy(
            src_ref=stage.at[slot, pair], dst_ref=back.at[slot, pair],
            send_sem=ret_send.at[slot, pair], recv_sem=ret_recv.at[slot, pair],
            device_id={"row": across, "col": c}, device_id_type=MESH,
        )

    def sums(which, slot, pair, put):
        acc = [[None, None] for _ in range(rows)]
        for kc in range(2):
            wide = right[slot, kc, pl.ds(pair * 2 * cols, 2 * cols), :].astype(F32)
            for kt in range(0, cols, 8):
                r = [wide[j * cols + kt : j * cols + kt + 8] for j in range(2)]
                for i in range(rows):
                    l = left32[which, kc, i * cols + kt : i * cols + kt + 8, :]
                    for j in range(2):
                        term = l * r[j]
                        acc[i][j] = term if acc[i][j] is None else acc[i][j] + term
        for i in range(rows):
            for j in range(2):
                put(i, j, jnp.sum(acc[i][j], axis=0, keepdims=True))

    def place(i, j, slot, pair, side, value):
        comb[pl.ds(i * cols + (slot * 2 + side) * rows + pair * 2 + j, 1), :] = value

    @pl.loop(0, span)
    def _(t):
        zs = source(lax.rem(t + jnp.where((z >= low) & (z < low + span), span - 1, 0), span))
        slot = zs - low

        @pl.loop(0, pairs)
        def _(pair):
            for kc in range(2):
                @pl.when(jnp.logical_not(passes(zs)) & ((zs != z) | (c != kc)))
                def _(kc=kc):
                    for q in range(sub):
                        block(slot, kc, pair * sub + q, row).wait_recv()

            def put_stage(i, j, value):
                stage[slot, pair, j * rows + i : j * rows + i + 1, :] = value

            sums(1 - y, slot, pair, put_stage)
            sums(y, slot, pair, lambda i, j, value: place(i, j, slot, pair, y, value))
            ret_copy(slot, pair).start()

    @pl.loop(0, span)
    def _(t):
        slot = source(lax.rem(t + jnp.where((z >= low) & (z < low + span), span - 1, 0), span)) - low

        @pl.loop(0, pairs)
        def _(pair):
            ret_copy(slot, pair).wait_recv()
            for i in range(rows):
                for j in range(2):
                    got = back[slot, pair, j * rows + i : j * rows + i + 1, :]
                    place(i, j, slot, pair, 1 - y, got)

    loads[4].wait()
    tri = layer_norm(comb[...]).astype(BF16)
    update = jnp.dot(tri, wo_ref[...], preferred_element_type=F32) * gate[...]
    out_ref[...] = update.astype(BF16)

    for p in range(pairs):
        own_all(p, lambda copy: copy.wait_send())
    left_copy(y, c, 0, across, c).wait_send()
    left_copy(y, c, 1, row, 1 - c).wait_send()
    left_copy(1 - y, c, 2, row, 1 - c).wait_send()

    @pl.loop(0, span)
    def _(slot):
        @pl.when(passes(slot + low))
        def _():
            @pl.loop(0, chunks)
            def _(q):
                for kc in range(2):
                    block(slot, kc, q, row).wait_send()

        for pair in range(pairs):
            ret_copy(slot, pair).wait_send()


def per_device(n, pair_rep, proj_weight, gate_weight, out_weight):
    rows, cols, channels = pair_rep.shape
    hid = out_weight.shape[0]
    flat = rows * cols
    pairs = rows // 2
    sub = 1
    chunks = pairs * sub
    span = n // 4
    padded = -(-2 * rows // 8) * 8
    vmem = pl.BlockSpec(memory_space=pltpu.VMEM)
    dma = pltpu.SemaphoreType.DMA
    out = pl.pallas_call(
        functools.partial(kernel, n, rows, cols, pairs, sub),
        out_shape=pltpu.VMEM((flat, channels), BF16),
        in_specs=[pl.BlockSpec(memory_space=pl.ANY)] * 4,
        out_specs=vmem,
        scratch_shapes=[
            pltpu.VMEM((flat, channels), BF16),
            pltpu.VMEM((2, channels, 2 * hid), BF16),
            pltpu.VMEM((channels, channels), BF16),
            pltpu.VMEM((hid, channels), BF16),
            pltpu.VMEM((flat, channels), BF16),
            dma((5,)),
            pltpu.VMEM((flat, hid), BF16),
            pltpu.VMEM((span, 2, flat, hid), BF16),
            pltpu.VMEM((2, 2, flat, hid), BF16),
            pltpu.VMEM((2, 2, flat, hid), F32),
            pltpu.VMEM((flat, hid), F32),
            pltpu.VMEM((flat, channels), F32),
            pltpu.VMEM((span, pairs, padded, hid), F32),
            pltpu.VMEM((span, pairs, padded, hid), F32),
            dma((3, chunks)),
            dma((span, 2, chunks)),
            dma((span, 2, chunks)),
            dma((3,)),
            dma((2, 2)),
            dma((span, pairs)),
            dma((span, pairs)),
        ],
        compiler_params=pltpu.CompilerParams(
            collective_id=0, has_side_effects=True, vmem_limit_bytes=60 * 1024 * 1024
        ),
    )(pair_rep.reshape(flat, channels), proj_weight, gate_weight, out_weight)
    return out.reshape(rows, cols, channels)


def solution(mesh):
    placed = (P(("groups", "row"), "col", None), P(), P(), P())
    return jax.shard_map(
        functools.partial(per_device, mesh.shape["row"]),
        mesh=mesh,
        in_specs=placed,
        out_specs=P(("groups", "row"), "col", None),
        check_vma=False,
    )
```

profile of v0, /device:TPU:1, one launch (start us, length us, event | category | flops | bytes accessed | tf_op | source)
XLA Modules:
  0.0 17.8 jit_solution(6772698709418597086)
XLA Ops:
  0.0 17.1 %shard_map.46 = bf16[400,128]{1,0:T(8,128)(2,1)S(1)} custom-call(bf16[400,128]{1,0:T(8,128)(2,1)} %bitcast.3, bf16[128,512]{1,0:T(8,128)(2,1)} %wp_hbm.1, bf16[128,128]{1,0:T(8,128)(2,1)} %wg_hbm.1, bf16[128,128]{1,0:T(8,128)(2,1)} %wo_hbm.1), custom_call_target="tpu_custom_call" | custom-call | tf_op jit(solution)/shard_map/pallas_call | solution.py:258
  17.2 0.6 %copy.6 = bf16[10,40,128]{2,1,0:T(8,128)(2,1)} copy(bf16[10,40,128]{2,1,0:T(8,128)(2,1)S(1)} %bitcast.2) | data formatting | bytes 204800
where the time goes:
time: 17.9 us; the launch traced here: 17.8 us
  Pallas kernels  17.1 us (96%)
  local copies, waits for them, and re-layouts  0.64 us (4%)
    pallas_call x1, Pallas kernels, per_device(): pl.pallas_call(functools.partial(kernel, n, rows, cols, pairs, sub), out_...  17.1 us
    unnamed x1, local copies, waits for them, and re-layouts  0.64 us

commit v1 on v0

v1 whole, which is shorter than its diff:
```python
import functools

import jax
import jax.numpy as jnp
from jax import lax
from jax.experimental import pallas as pl
from jax.experimental.pallas import tpu as pltpu
from jax.sharding import PartitionSpec as P

MESH = pl.DeviceIdType.MESH
F32 = jnp.float32
BF16 = jnp.bfloat16


def layer_norm(values):
    average = jnp.mean(values, axis=-1, keepdims=True)
    centered = values - average
    spread = jnp.mean(centered * centered, axis=-1, keepdims=True)
    return centered * lax.rsqrt(spread + 1e-05)


def kernel(
    n, rows, cols, pairs, x_hbm, wp_hbm, wg_hbm, wo_hbm, out_ref,
    x_ref, wp_ref, wg_ref, wo_ref, normed, in_sem, own, right, left, left32, comb, gate, stage, back,
    own_send, fwd_send, recv, lsend, lrecv, ret_send, ret_recv,
):
    hid = wo_ref.shape[0]
    flat = rows * cols
    step = flat // pairs
    loads = [pltpu.make_async_copy(x_hbm, x_ref, in_sem.at[0])]
    for k in (1, 0):
        cut = (slice(None), pl.ds(2 * hid * k, 2 * hid))
        loads.append(pltpu.make_async_copy(wp_hbm.at[cut], wp_ref.at[k], in_sem.at[len(loads)]))
    loads.append(pltpu.make_async_copy(wg_hbm, wg_ref, in_sem.at[3]))
    loads.append(pltpu.make_async_copy(wo_hbm, wo_ref, in_sem.at[4]))
    for load in loads:
        load.start()
    deep = n // 2
    span = deep // 2
    row, c = lax.axis_index("row"), lax.axis_index("col")
    z, y = row // 2, row % 2
    across = 2 * z + 1 - y
    has_up, has_down, has_far = z < deep - 1, z > 0, z > 2
    low = c * span
    dest = z // span
    my_slot = z - dest * span
    barrier = pltpu.get_barrier_semaphore()

    def greet(r, cc):
        pl.semaphore_signal(barrier, inc=1, device_id={"row": r, "col": cc}, device_id_type=MESH)

    @pl.when((z + 3 < deep) & ((z + 3) // span == c))
    def _():
        for cc in range(2):
            greet(row + 6, cc)

    @pl.when(has_up)
    def _():
        for cc in range(2):
            greet(row + 2, cc)

    @pl.when(has_down)
    def _():
        for cc in range(2):
            greet(row - 2, cc)

    greet(across, c)
    greet(row, 1 - c)

    def gated(values, k):
        proj = jnp.dot(values, wp_ref[k], preferred_element_type=F32)
        return (jax.nn.sigmoid(proj[:, :hid]) * proj[:, hid:]).astype(BF16)

    def prepare(p):
        here = pl.ds(p * step, step)
        values = layer_norm(x_ref[here, :].astype(F32)).astype(BF16)
        normed[here, :] = values
        own[here, :] = gated(values, 1)

    loads[0].wait()
    loads[1].wait()

    ways = ((0, has_far, row - 6, dest), (1, has_up, row + 2, dest), (2, has_down, row - 2, dest), (3, dest != c, row, dest))

    def own_copy(way, r, cc, part):
        return pltpu.make_async_remote_copy(
            src_ref=own.at[part], dst_ref=right.at[my_slot, c, part],
            send_sem=own_send.at[way], recv_sem=recv.at[my_slot, part.start // step],
            device_id={"row": r, "col": cc}, device_id_type=MESH,
        )

    for p in range(pairs):
        prepare(p)
    def compute_left():
        loads[2].wait()
        left[y, c] = gated(normed[...], 0)

    @pl.when(has_up)
    def _():
        compute_left()
    pl.semaphore_wait(barrier, 2 + 2 * has_up.astype(jnp.int32) + 2 * has_down.astype(jnp.int32) + has_far.astype(jnp.int32))
    for p in range(pairs):
        for way, cond, r, cc in ways:
            @pl.when(cond)
            def _(way=way, r=r, cc=cc):
                own_copy(way, r, cc, pl.ds(p * step, step)).start()

    @pl.when(dest == c)
    def _():
        right[my_slot, c] = own[...]

    def left_copy(which, kc, way, arrive, r, cc):
        part = left.at[which, kc]
        return pltpu.make_async_remote_copy(
            src_ref=part, dst_ref=part, send_sem=lsend.at[way], recv_sem=lrecv.at[arrive],
            device_id={"row": r, "col": cc}, device_id_type=MESH,
        )

    to_across = left_copy(y, c, 0, 0, across, c)
    to_sibling = left_copy(y, c, 1, 1, row, 1 - c)
    passed_on = left_copy(1 - y, c, 2, 1, row, 1 - c)
    @pl.when(jnp.logical_not(has_up))
    def _():
        compute_left()
    to_across.start()
    to_sibling.start()
    left32[y, c] = left[y, c].astype(F32)
    loads[3].wait()
    gate[...] = jax.nn.sigmoid(jnp.dot(normed[...], wg_ref[...], preferred_element_type=F32))

    def source(t):
        inside = low + lax.rem(z - low + t + 1 + deep, span)
        return jnp.where(z < low, low + t, jnp.where(z >= low + span, low + span - 1 - t, inside))

    def passes(zs):
        return ((zs < z) & has_up) | (((zs == z + 1) | (zs > z + 2)) & has_down)

    def block(part, slot, q, r):
        return pltpu.make_async_remote_copy(
            src_ref=part, dst_ref=part, send_sem=fwd_send.at[slot],
            recv_sem=recv.at[slot, q], device_id={"row": r, "col": c}, device_id_type=MESH,
        )

    def both(slot, q):
        return right.at[slot, :, pl.ds(q * step, step)]

    def send_on(t, start, stop):
        zs = source(t)
        slot = zs - low

        @pl.when(passes(zs))
        def _():
            @pl.loop(start, stop)
            def _(q):
                block(both(slot, q), slot, q, row).wait_recv()
                block(both(slot, q), slot, q, jnp.where(zs < z, row + 2, row - 2)).start()

    early = jnp.where(c == 0, pairs, pairs - 2)
    send_on(0, 0, early)
    left_copy(1 - y, c, 0, 0, across, c).wait_recv()
    passed_on.start()
    send_on(0, early, pairs)
    pl.loop(1, span)(lambda t: send_on(t, 0, pairs))
    left32[1 - y, c] = left[1 - y, c].astype(F32)
    pltpu.make_async_remote_copy(
        src_ref=left.at[:, 1 - c], dst_ref=left.at[:, 1 - c], send_sem=lsend.at[1], recv_sem=lrecv.at[1],
        device_id={"row": row, "col": 1 - c}, device_id_type=MESH,
    ).wait_recv()
    for which in range(2):
        left32[which, 1 - c] = left[which, 1 - c].astype(F32)

    def ret_copy(part, there, slot):
        return pltpu.make_async_remote_copy(
            src_ref=part, dst_ref=there, send_sem=ret_send, recv_sem=ret_recv.at[slot],
            device_id={"row": across, "col": c}, device_id_type=MESH,
        )

    def sums(which, slot, pair, put):
        acc = [[None, None] for _ in range(rows)]
        for kc in range(2):
            wide = right[slot, kc, pl.ds(pair * 2 * cols, 2 * cols), :].astype(F32)
            for kt in range(0, cols, 8):
                r = [wide[j * cols + kt : j * cols + kt + 8] for j in range(2)]
                for i in range(rows):
                    l = left32[which, kc, i * cols + kt : i * cols + kt + 8, :]
                    for j in range(2):
                        term = l * r[j]
                        acc[i][j] = term if acc[i][j] is None else acc[i][j] + term
        for i in range(rows):
            for j in range(2):
                put(i, j, jnp.sum(acc[i][j], axis=0, keepdims=True))

    def place(i, j, slot, pair, side, value):
        comb[pl.ds(i * cols + (slot * 2 + side) * rows + pair * 2 + j, 1), :] = value

    def order(t):
        return source(lax.rem(t + jnp.where((z >= low) & (z < low + span), span - 1, 0), span))

    @pl.loop(0, pairs)
    def _(pair):
        @pl.loop(0, span)
        def _(t):
            zs = order(t)
            slot = zs - low
            @pl.when((zs == z) & jnp.logical_not(passes(zs)))
            def _():
                block(right.at[slot, 1 - c, pl.ds(pair * step, step)], slot, pair, row).wait_recv()

            @pl.when((zs != z) & jnp.logical_not(passes(zs)))
            def _():
                block(both(slot, pair), slot, pair, row).wait_recv()

            def put_stage(i, j, value):
                stage[slot, pair, j * rows + i : j * rows + i + 1, :] = value

            sums(1 - y, slot, pair, put_stage)
            ret_copy(stage.at[slot, pair], back.at[slot, pair], slot).start()
            sums(y, slot, pair, lambda i, j, value: place(i, j, slot, pair, y, value))

    for way, cond, r, cc in ways:
        @pl.when(cond)
        def _(way=way, r=r, cc=cc):
            own_copy(way, r, cc, pl.ds(0, flat)).wait_send()
    for copy in (to_across, to_sibling, passed_on):
        copy.wait_send()

    @pl.loop(0, span)
    def _(slot):
        @pl.when(passes(slot + low))
        def _():
            block(right.at[slot], slot, 0, row).wait_send()

    @pl.loop(0, span)
    def _(t):
        slot = order(t) - low
        ret_copy(stage.at[slot], back.at[slot], slot).wait_recv()

        @pl.loop(0, pairs)
        def _(pair):
            for i in range(rows):
                for j in range(2):
                    got = back[slot, pair, j * rows + i : j * rows + i + 1, :]
                    place(i, j, slot, pair, 1 - y, got)

    ret_copy(stage, back, 0).wait_send()
    loads[4].wait()
    tri = layer_norm(comb[...]).astype(BF16)
    update = jnp.dot(tri, wo_ref[...], preferred_element_type=F32) * gate[...]
    out_ref[...] = update.astype(BF16)


def per_device(n, pair_rep, proj_weight, gate_weight, out_weight):
    rows, cols, channels = pair_rep.shape
    hid = out_weight.shape[0]
    flat = rows * cols
    pairs = rows // 2
    span = n // 4
    padded = -(-2 * rows // 8) * 8
    vmem = pl.BlockSpec(memory_space=pltpu.VMEM)
    dma = pltpu.SemaphoreType.DMA
    out = pl.pallas_call(
        functools.partial(kernel, n, rows, cols, pairs),
        out_shape=pltpu.VMEM((flat, channels), BF16),
        in_specs=[pl.BlockSpec(memory_space=pl.ANY)] * 4,
        out_specs=vmem,
        scratch_shapes=[
            pltpu.VMEM((flat, channels), BF16),
            pltpu.VMEM((2, channels, 2 * hid), BF16),
            pltpu.VMEM((channels, channels), BF16),
            pltpu.VMEM((hid, channels), BF16),
            pltpu.VMEM((flat, channels), BF16),
            dma((5,)),
            pltpu.VMEM((flat, hid), BF16),
            pltpu.VMEM((span, 2, flat, hid), BF16),
            pltpu.VMEM((2, 2, flat, hid), BF16),
            pltpu.VMEM((2, 2, flat, hid), F32),
            pltpu.VMEM((flat, hid), F32),
            pltpu.VMEM((flat, channels), F32),
            pltpu.VMEM((span, pairs, padded, hid), F32),
            pltpu.VMEM((span, pairs, padded, hid), F32),
            dma((4,)),
            dma((span,)),
            dma((span, pairs)),
            dma((3,)),
            dma((2,)),
            dma,
            dma((span,)),
        ],
        compiler_params=pltpu.CompilerParams(
            collective_id=0, has_side_effects=True, vmem_limit_bytes=60 * 1024 * 1024
        ),
    )(pair_rep.reshape(flat, channels), proj_weight, gate_weight, out_weight)
    return out.reshape(rows, cols, channels)


def solution(mesh):
    placed = (P(("groups", "row"), "col", None), P(), P(), P())
    return jax.shard_map(
        functools.partial(per_device, mesh.shape["row"]),
        mesh=mesh,
        in_specs=placed,
        out_specs=P(("groups", "row"), "col", None),
        check_vma=False,
    )
```

time: 17.9 us -> 16.4 us (0.916)
  Pallas kernels: 17.1 us -> 15.6 us
    pallas_call x1, Pallas kernels: 17.1 us -> 15.6 us  [per_device(): pl.pallas_call(functools.partial(kernel, n, rows, cols, pairs), out_shape...]
where the time goes in v1:
time: 16.4 us; the launch traced here: 16.3 us
  Pallas kernels  15.6 us (95%)
  local copies, waits for them, and re-layouts  0.64 us (4%)
    pallas_call x1, Pallas kernels, per_device(): pl.pallas_call(functools.partial(kernel, n, rows, cols, pairs), out_shape...  15.6 us
    unnamed x1, local copies, waits for them, and re-layouts  0.64 us

profile of v1, /device:TPU:1, one launch (start us, length us, event | category | flops | bytes accessed | tf_op | source)
XLA Modules:
  0.0 16.3 jit_solution(1076394412252980373)
XLA Ops:
  0.0 15.6 %shard_map.46 = bf16[400,128]{1,0:T(8,128)(2,1)S(1)} custom-call(bf16[400,128]{1,0:T(8,128)(2,1)} %bitcast.3, bf16[128,512]{1,0:T(8,128)(2,1)} %wp_hbm.1, bf16[128,128]{1,0:T(8,128)(2,1)} %wg_hbm.1, bf16[128,128]{1,0:T(8,128)(2,1)} %wo_hbm.1), custom_call_target="tpu_custom_call" | custom-call | tf_op jit(solution)/shard_map/pallas_call | solution.py:261
  15.6 0.6 %copy.6 = bf16[10,40,128]{2,1,0:T(8,128)(2,1)} copy(bf16[10,40,128]{2,1,0:T(8,128)(2,1)S(1)} %bitcast.2) | data formatting | bytes 204800

commit v2 on v1

--- a/solution.py
+++ b/solution.py
@@ -20,9 +20,9 @@
 
 
 def kernel(
-    n, rows, cols, pairs, x_hbm, wp_hbm, wg_hbm, wo_hbm, out_ref,
-    x_ref, wp_ref, wg_ref, wo_ref, normed, in_sem, own, right, left, left32, comb, gate, stage, back,
-    own_send, fwd_send, recv, lsend, lrecv, ret_send, ret_recv,
+    n, rows, cols, pairs, twice, x_hbm, wp_hbm, wg_hbm, wo_hbm, out_ref,
+    x_ref, wp_ref, wg_ref, wo_ref, normed, in_sem, own, right, left, left32, comb, gate, stage, back, other,
+    own_send, fwd_send, recv, lsend, lrecv, ret_send, ret_recv, other_send, other_recv,
 ):
     hid = wo_ref.shape[0]
     flat = rows * cols
@@ -44,6 +44,11 @@
     low = c * span
     dest = z // span
     my_slot = z - dest * span
+    once = pairs - twice
+    far = (z < low) | (z >= low + span)
+    helped = far & (y == 0)
+    target = z + 1 - 2 * c
+    helps = (y == 1) & jnp.where(c == 1, (z >= 1) & (z <= span), (z >= span - 1) & (z < deep - 1))
     barrier = pltpu.get_barrier_semaphore()
 
     def greet(r, cc):
@@ -63,6 +68,10 @@
     def _():
         for cc in range(2):
             greet(row - 2, cc)
+
+    @pl.when(helped)
+    def _():
+        greet(2 * (z - 1 + 2 * c) + 1, c)
 
     greet(across, c)
     greet(row, 1 - c)
@@ -98,7 +107,7 @@
     @pl.when(has_up)
     def _():
         compute_left()
-    pl.semaphore_wait(barrier, 2 + 2 * has_up.astype(jnp.int32) + 2 * has_down.astype(jnp.int32) + has_far.astype(jnp.int32))
+    pl.semaphore_wait(barrier, 2 + 2 * has_up.astype(jnp.int32) + 2 * has_down.astype(jnp.int32) + has_far.astype(jnp.int32) + helps.astype(jnp.int32))
     for p in range(pairs):
         for way, cond, r, cc in ways:
             @pl.when(cond)
@@ -126,7 +135,8 @@
     to_sibling.start()
     left32[y, c] = left[y, c].astype(F32)
     loads[3].wait()
-    gate[...] = jax.nn.sigmoid(jnp.dot(normed[...], wg_ref[...], preferred_element_type=F32))
+    opened = jax.nn.sigmoid(jnp.dot(normed[...], wg_ref[...], preferred_element_type=F32))
+    gate[...] = opened.reshape(rows, cols, -1)
 
     def source(t):
         inside = low + lax.rem(z - low + t + 1 + deep, span)
@@ -143,6 +153,15 @@
 
     def both(slot, q):
         return right.at[slot, :, pl.ds(q * step, step)]
+
+    def other_copy(slot, d, count):
+        return pltpu.make_async_remote_copy(
+            src_ref=right.at[slot, :, pl.ds((once + d) * step, count * step)],
+            dst_ref=other.at[:, pl.ds(d * step, count * step)],
+            send_sem=other_send, recv_sem=other_recv.at[d], device_id={"row": 2 * target, "col": c}, device_id_type=MESH,
+        )
+
+    shared = jnp.where(c == 1, jnp.where(target == 0, span, deep - 1), 0)
 
     def send_on(t, start, stop):
         zs = source(t)
@@ -153,9 +172,13 @@
             @pl.loop(start, stop)
             def _(q):
                 block(both(slot, q), slot, q, row).wait_recv()
+                @pl.when(helps & (zs == shared) & (q >= once))
+                def _():
+                    other_copy(slot, q - once, 1).start()
+
                 block(both(slot, q), slot, q, jnp.where(zs < z, row + 2, row - 2)).start()
 
-    early = jnp.where(c == 0, pairs, pairs - 2)
+    early = jnp.where(c == 0, pairs, 0)
     send_on(0, 0, early)
     left_copy(1 - y, c, 0, 0, across, c).wait_recv()
     passed_on.start()
@@ -171,14 +194,14 @@
 
     def ret_copy(part, there, slot):
         return pltpu.make_async_remote_copy(
-            src_ref=part, dst_ref=there, send_sem=ret_send, recv_sem=ret_recv.at[slot],
+            src_ref=part, dst_ref=there, send_sem=ret_send.at[slot], recv_sem=ret_recv.at[slot],
             device_id={"row": across, "col": c}, device_id_type=MESH,
         )
 
-    def sums(which, slot, pair, put):
+    def sums(which, blocks, pair, put):
         acc = [[None, None] for _ in range(rows)]
         for kc in range(2):
-            wide = right[slot, kc, pl.ds(pair * 2 * cols, 2 * cols), :].astype(F32)
+            wide = blocks[kc, pl.ds(pair * 2 * cols, 2 * cols), :].astype(F32)
             for kt in range(0, cols, 8):
                 r = [wide[j * cols + kt : j * cols + kt + 8] for j in range(2)]
                 for i in range(rows):
@@ -191,17 +214,22 @@
                 put(i, j, jnp.sum(acc[i][j], axis=0, keepdims=True))
 
     def place(i, j, slot, pair, side, value):
-        comb[pl.ds(i * cols + (slot * 2 + side) * rows + pair * 2 + j, 1), :] = value
+        comb[i, pl.ds((slot * 2 + side) * rows + pair * 2 + j, 1), :] = value
 
     def order(t):
-        return source(lax.rem(t + jnp.where((z >= low) & (z < low + span), span - 1, 0), span))
-
-    @pl.loop(0, pairs)
-    def _(pair):
-        @pl.loop(0, span)
-        def _(t):
-            zs = order(t)
-            slot = zs - low
+        inside = lax.rem(t + span - 1, span)
+        return source(jnp.where((z >= low) & (z < low + span), inside, jnp.where(z > 0, t, span - 1 - t)))
+
+    last = order(span - 1) - low
+
+    @pl.loop(0, span)
+    def _(t):
+        zs = order(t)
+        slot = zs - low
+        kept = jnp.where(far & (y == 1) & (slot == last), once, pairs)
+
+        @pl.loop(0, pairs)
+        def _(pair):
             @pl.when((zs == z) & jnp.logical_not(passes(zs)))
             def _():
                 block(right.at[slot, 1 - c, pl.ds(pair * step, step)], slot, pair, row).wait_recv()
@@ -213,9 +241,13 @@
             def put_stage(i, j, value):
                 stage[slot, pair, j * rows + i : j * rows + i + 1, :] = value
 
-            sums(1 - y, slot, pair, put_stage)
-            ret_copy(stage.at[slot, pair], back.at[slot, pair], slot).start()
-            sums(y, slot, pair, lambda i, j, value: place(i, j, slot, pair, y, value))
+            @pl.when(pair < kept)
+            def _():
+                sums(1 - y, right.at[slot], pair, put_stage)
+                ret_copy(stage.at[slot, pair], back.at[slot, pair], slot).start()
+
+            sums(y, right.at[slot], pair, lambda i, j, value: place(i, j, slot, pair, y, value))
+
 
     for way, cond, r, cc in ways:
         @pl.when(cond)
@@ -230,23 +262,60 @@
         def _():
             block(right.at[slot], slot, 0, row).wait_send()
 
-    @pl.loop(0, span)
-    def _(t):
-        slot = order(t) - low
-        ret_copy(stage.at[slot], back.at[slot], slot).wait_recv()
-
-        @pl.loop(0, pairs)
+    @pl.when(helps)
+    def _():
+        other_copy(shared - low, 0, twice).wait_send()
+
+    def collect(slot, part, stop):
+        ret_copy(stage.at[slot, part], back.at[slot, part], slot).wait_recv()
+
+        @pl.loop(0, stop)
         def _(pair):
             for i in range(rows):
                 for j in range(2):
                     got = back[slot, pair, j * rows + i : j * rows + i + 1, :]
                     place(i, j, slot, pair, 1 - y, got)
 
-    ret_copy(stage, back, 0).wait_send()
-    loads[4].wait()
-    tri = layer_norm(comb[...]).astype(BF16)
-    update = jnp.dot(tri, wo_ref[...], preferred_element_type=F32) * gate[...]
-    out_ref[...] = update.astype(BF16)
+    def finish(start, width):
+        here = (slice(None), pl.ds(pl.multiple_of(start, 8), width))
+        tri = layer_norm(comb[here].reshape(rows * width, hid)).astype(BF16)
+        update = jnp.dot(tri, wo_ref[...], preferred_element_type=F32) * gate[here].reshape(rows * width, -1)
+        out_ref[here] = update.astype(BF16).reshape(rows, width, -1)
+
+    wide = 2 * rows
+    width = max(-(-(s * wide % 8 + wide) // 8) * 8 for s in range(span))
+    start = jnp.minimum(last * wide // 8 * 8, cols - width)
+    every = pl.ds(0, pairs)
+    some = pl.ds(0, once)
+
+    @pl.loop(0, twice)
+    def _(d):
+        @pl.when(d == twice - 1)
+        def _():
+            pl.loop(0, span - 1)(lambda t: collect(order(t) - low, every, pairs))
+            loads[4].wait()
+            if span == 2:
+                finish(jnp.where(start == 0, width, 0), cols - width)
+            else:
+                @pl.loop(0, cols // 8)
+                def _(b):
+                    @pl.when((8 * b < start) | (8 * b >= start + width))
+                    def _():
+                        finish(8 * b, 8)
+
+        @pl.when(helped)
+        def _():
+            other_copy(last, d, 1).wait_recv()
+            sums(y, other, d, lambda i, j, value: place(i, j, last, once + d, 1 - y, value))
+
+    pl.when(helped)(lambda: collect(last, some, once))
+    pl.when(jnp.logical_not(helped))(lambda: collect(last, every, pairs))
+    finish(start, width)
+    @pl.loop(0, span)
+    def _(slot):
+        kept = far & (y == 1) & (slot == last)
+        pl.when(kept)(lambda: ret_copy(stage.at[slot, some], back.at[slot, some], slot).wait_send())
+        pl.when(jnp.logical_not(kept))(lambda: ret_copy(stage.at[slot], back.at[slot], slot).wait_send())
 
 
 def per_device(n, pair_rep, proj_weight, gate_weight, out_weight):
@@ -254,13 +323,14 @@
     hid = out_weight.shape[0]
     flat = rows * cols
     pairs = rows // 2
+    twice = pairs // 2
     span = n // 4
     padded = -(-2 * rows // 8) * 8
     vmem = pl.BlockSpec(memory_space=pltpu.VMEM)
     dma = pltpu.SemaphoreType.DMA
-    out = pl.pallas_call(
-        functools.partial(kernel, n, rows, cols, pairs),
-        out_shape=pltpu.VMEM((flat, channels), BF16),
+    return pl.pallas_call(
+        functools.partial(kernel, n, rows, cols, pairs, twice),
+        out_shape=pltpu.VMEM((rows, cols, channels), BF16),
         in_specs=[pl.BlockSpec(memory_space=pl.ANY)] * 4,
         out_specs=vmem,
         scratch_shapes=[
@@ -274,23 +344,25 @@
             pltpu.VMEM((span, 2, flat, hid), BF16),
             pltpu.VMEM((2, 2, flat, hid), BF16),
             pltpu.VMEM((2, 2, flat, hid), F32),
-            pltpu.VMEM((flat, hid), F32),
-            pltpu.VMEM((flat, channels), F32),
+            pltpu.VMEM((rows, cols, hid), F32),
+            pltpu.VMEM((rows, cols, channels), F32),
             pltpu.VMEM((span, pairs, padded, hid), F32),
             pltpu.VMEM((span, pairs, padded, hid), F32),
+            pltpu.VMEM((2, twice * (flat // pairs), hid), BF16),
             dma((4,)),
             dma((span,)),
             dma((span, pairs)),
             dma((3,)),
             dma((2,)),
+            dma((span,)),
+            dma((span,)),
             dma,
-            dma((span,)),
+            dma((twice,)),
         ],
         compiler_params=pltpu.CompilerParams(
             collective_id=0, has_side_effects=True, vmem_limit_bytes=60 * 1024 * 1024
         ),
     )(pair_rep.reshape(flat, channels), proj_weight, gate_weight, out_weight)
-    return out.reshape(rows, cols, channels)
 
 
 def solution(mesh):

time: 16.4 us -> 15.3 us (0.933)
  Pallas kernels: 15.6 us -> 14.5 us
    pallas_call x1, Pallas kernels: 15.6 us -> 14.5 us  [per_device(): pl.pallas_call(functools.partial(kernel, n, rows, cols, pairs, twice), ou...]
where the time goes in v2:
time: 15.3 us; the launch traced here: 15.2 us
  Pallas kernels  14.5 us (95%)
  local copies, waits for them, and re-layouts  0.64 us (4%)
    pallas_call x1, Pallas kernels, per_device(): pl.pallas_call(functools.partial(kernel, n, rows, cols, pairs, twice), ou...  14.5 us
    unnamed x1, local copies, waits for them, and re-layouts  0.64 us

profile of v2, /device:TPU:1, one launch (start us, length us, event | category | flops | bytes accessed | tf_op | source)
XLA Modules:
  0.0 15.2 jit_solution(10981979645175680753)
XLA Ops:
  0.0 14.5 %shard_map.46 = bf16[10,40,128]{2,1,0:T(8,128)(2,1)S(1)} custom-call(bf16[400,128]{1,0:T(8,128)(2,1)} %bitcast.1, bf16[128,512]{1,0:T(8,128)(2,1)} %wp_hbm.1, bf16[128,128]{1,0:T(8,128)(2,1)} %wg_hbm.1, bf16[128,128]{1,0:T(8,128)(2,1)} %wo_hbm.1), custom_call_target="tpu_custom_call" | custom-call | tf_op jit(solution)/shard_map/pallas_call | solution.py:331
  14.5 0.6 %copy.6 = bf16[10,40,128]{2,1,0:T(8,128)(2,1)} copy(bf16[10,40,128]{2,1,0:T(8,128)(2,1)S(1)} %shard_map.46) | data formatting | bytes 204800

commit v3 on v2

--- a/solution.py
+++ b/solution.py
@@ -10,6 +10,8 @@
 MESH = pl.DeviceIdType.MESH
 F32 = jnp.float32
 BF16 = jnp.bfloat16
+TWICE = 3
+LESS = 2
 
 
 def layer_norm(values):
@@ -44,8 +46,12 @@
     low = c * span
     dest = z // span
     my_slot = z - dest * span
-    once = pairs - twice
     far = (z < low) | (z >= low + span)
+
+    def first_twice(chip):
+        return pairs - jnp.where((chip == 0) & (c == 1), twice, LESS)
+
+    once = first_twice(z)
     helped = far & (y == 0)
     target = z + 1 - 2 * c
     helps = (y == 1) & jnp.where(c == 1, (z >= 1) & (z <= span), (z >= span - 1) & (z < deep - 1))
@@ -102,7 +108,7 @@
         prepare(p)
     def compute_left():
         loads[2].wait()
-        left[y, c] = gated(normed[...], 0)
+        left[2 * c + y] = gated(normed[...], 0)
 
     @pl.when(has_up)
     def _():
@@ -118,22 +124,22 @@
     def _():
         right[my_slot, c] = own[...]
 
-    def left_copy(which, kc, way, arrive, r, cc):
-        part = left.at[which, kc]
-        return pltpu.make_async_remote_copy(
-            src_ref=part, dst_ref=part, send_sem=lsend.at[way], recv_sem=lrecv.at[arrive],
+    def left_copy(which, kc, arrive, r, cc):
+        part = left.at[2 * kc + which]
+        return pltpu.make_async_remote_copy(
+            src_ref=part, dst_ref=part, send_sem=lsend, recv_sem=lrecv.at[arrive],
             device_id={"row": r, "col": cc}, device_id_type=MESH,
         )
 
-    to_across = left_copy(y, c, 0, 0, across, c)
-    to_sibling = left_copy(y, c, 1, 1, row, 1 - c)
-    passed_on = left_copy(1 - y, c, 2, 1, row, 1 - c)
+    to_across = left_copy(y, c, 0, across, c)
+    to_sibling = left_copy(y, c, 1, row, 1 - c)
+    passed_on = left_copy(1 - y, c, 1, row, 1 - c)
     @pl.when(jnp.logical_not(has_up))
     def _():
         compute_left()
     to_across.start()
     to_sibling.start()
-    left32[y, c] = left[y, c].astype(F32)
+    left32[y, c] = left[2 * c + y].astype(F32)
     loads[3].wait()
     opened = jax.nn.sigmoid(jnp.dot(normed[...], wg_ref[...], preferred_element_type=F32))
     gate[...] = opened.reshape(rows, cols, -1)
@@ -156,41 +162,50 @@
 
     def other_copy(slot, d, count):
         return pltpu.make_async_remote_copy(
-            src_ref=right.at[slot, :, pl.ds((once + d) * step, count * step)],
+            src_ref=right.at[slot, :, pl.ds((once_there + d) * step, count * step)],
             dst_ref=other.at[:, pl.ds(d * step, count * step)],
             send_sem=other_send, recv_sem=other_recv.at[d], device_id={"row": 2 * target, "col": c}, device_id_type=MESH,
         )
 
+    once_there = first_twice(target)
     shared = jnp.where(c == 1, jnp.where(target == 0, span, deep - 1), 0)
 
-    def send_on(t, start, stop):
-        zs = source(t)
+    def relay(zs, q):
         slot = zs - low
+        to = jnp.where(zs < z, row + 2, row - 2)
 
         @pl.when(passes(zs))
         def _():
-            @pl.loop(start, stop)
-            def _(q):
-                block(both(slot, q), slot, q, row).wait_recv()
-                @pl.when(helps & (zs == shared) & (q >= once))
-                def _():
-                    other_copy(slot, q - once, 1).start()
-
-                block(both(slot, q), slot, q, jnp.where(zs < z, row + 2, row - 2)).start()
+            doubled = helps & (zs == shared) & (q >= once_there)
+            block(both(slot, q), slot, q, row).wait_recv()
+
+            @pl.when(doubled)
+            def _():
+                other_copy(slot, q - once_there, 1).start()
+
+            @pl.when(jnp.logical_not(doubled))
+            def _():
+                block(both(slot, q), slot, q, to).start()
+
+            @pl.when(doubled & (q == pairs - 1))
+            def _():
+                pl.loop(once_there, pairs)(lambda p: block(both(slot, p), slot, p, to).start())
 
     early = jnp.where(c == 0, pairs, 0)
-    send_on(0, 0, early)
-    left_copy(1 - y, c, 0, 0, across, c).wait_recv()
+    pl.loop(0, early)(lambda q: relay(source(0), q))
+    left_copy(1 - y, c, 0, across, c).wait_recv()
     passed_on.start()
-    send_on(0, early, pairs)
-    pl.loop(1, span)(lambda t: send_on(t, 0, pairs))
-    left32[1 - y, c] = left[1 - y, c].astype(F32)
-    pltpu.make_async_remote_copy(
-        src_ref=left.at[:, 1 - c], dst_ref=left.at[:, 1 - c], send_sem=lsend.at[1], recv_sem=lrecv.at[1],
-        device_id={"row": row, "col": 1 - c}, device_id_type=MESH,
-    ).wait_recv()
-    for which in range(2):
-        left32[which, 1 - c] = left[which, 1 - c].astype(F32)
+    pl.loop(early, pairs)(lambda q: relay(source(0), q))
+
+    def take_left():
+        left32[1 - y, c] = left[2 * c + 1 - y].astype(F32)
+        theirs = left.at[pl.ds(2 * (1 - c), 2)]
+        pltpu.make_async_remote_copy(
+            src_ref=theirs, dst_ref=theirs, send_sem=lsend, recv_sem=lrecv.at[1],
+            device_id={"row": row, "col": 1 - c}, device_id_type=MESH,
+        ).wait_recv()
+        for which in range(2):
+            left32[which, 1 - c] = left[2 * (1 - c) + which].astype(F32)
 
     def ret_copy(part, there, slot):
         return pltpu.make_async_remote_copy(
@@ -222,39 +237,52 @@
 
     last = order(span - 1) - low
 
-    @pl.loop(0, span)
-    def _(t):
-        zs = order(t)
+    lead = pairs // 2
+
+    def combine(index):
+        zs = order(index // pairs)
+        pair = index % pairs
         slot = zs - low
         kept = jnp.where(far & (y == 1) & (slot == last), once, pairs)
-
-        @pl.loop(0, pairs)
-        def _(pair):
-            @pl.when((zs == z) & jnp.logical_not(passes(zs)))
-            def _():
-                block(right.at[slot, 1 - c, pl.ds(pair * step, step)], slot, pair, row).wait_recv()
-
-            @pl.when((zs != z) & jnp.logical_not(passes(zs)))
-            def _():
-                block(both(slot, pair), slot, pair, row).wait_recv()
-
-            def put_stage(i, j, value):
-                stage[slot, pair, j * rows + i : j * rows + i + 1, :] = value
-
-            @pl.when(pair < kept)
-            def _():
-                sums(1 - y, right.at[slot], pair, put_stage)
-                ret_copy(stage.at[slot, pair], back.at[slot, pair], slot).start()
-
-            sums(y, right.at[slot], pair, lambda i, j, value: place(i, j, slot, pair, y, value))
+        @pl.when((zs == z) & jnp.logical_not(passes(zs)))
+        def _():
+            block(right.at[slot, 1 - c, pl.ds(pair * step, step)], slot, pair, row).wait_recv()
+
+        @pl.when((zs != z) & jnp.logical_not(passes(zs)))
+        def _():
+            block(both(slot, pair), slot, pair, row).wait_recv()
+
+        def put_stage(i, j, value):
+            stage[slot, pair, j * rows + i : j * rows + i + 1, :] = value
+
+        @pl.when(pair < kept)
+        def _():
+            sums(1 - y, right.at[slot], pair, put_stage)
+            ret_copy(stage.at[slot, pair], back.at[slot, pair], slot).start()
+
+        sums(y, right.at[slot], pair, lambda i, j, value: place(i, j, slot, pair, y, value))
+
+    rate = 2 if span == 2 else 1
+
+    @pl.loop(0, -(-span * pairs // rate) + lead)
+    def _(index):
+        pl.when(index < (span - 1) * pairs)(lambda: relay(source(1 + index // pairs), index % pairs))
+        pl.when(index == lead)(take_left)
+
+        @pl.when(index >= lead)
+        def _():
+            pl.loop(rate * (index - lead), jnp.minimum(rate * (index - lead + 1), span * pairs))(combine)
 
 
     for way, cond, r, cc in ways:
         @pl.when(cond)
         def _(way=way, r=r, cc=cc):
             own_copy(way, r, cc, pl.ds(0, flat)).wait_send()
-    for copy in (to_across, to_sibling, passed_on):
-        copy.wait_send()
+    sent = left.at[pl.ds(0, 3)]
+    pltpu.make_async_remote_copy(
+        src_ref=sent, dst_ref=sent, send_sem=lsend, recv_sem=lrecv.at[1],
+        device_id={"row": row, "col": 1 - c}, device_id_type=MESH,
+    ).wait_send()
 
     @pl.loop(0, span)
     def _(slot):
@@ -262,9 +290,10 @@
         def _():
             block(right.at[slot], slot, 0, row).wait_send()
 
-    @pl.when(helps)
-    def _():
-        other_copy(shared - low, 0, twice).wait_send()
+    for count in (twice, LESS):
+        @pl.when(helps & (once_there == pairs - count))
+        def _(count=count):
+            other_copy(shared - low, 0, count).wait_send()
 
     def collect(slot, part, stop):
         ret_copy(stage.at[slot, part], back.at[slot, part], slot).wait_recv()
@@ -276,46 +305,40 @@
                     got = back[slot, pair, j * rows + i : j * rows + i + 1, :]
                     place(i, j, slot, pair, 1 - y, got)
 
-    def finish(start, width):
-        here = (slice(None), pl.ds(pl.multiple_of(start, 8), width))
-        tri = layer_norm(comb[here].reshape(rows * width, hid)).astype(BF16)
-        update = jnp.dot(tri, wo_ref[...], preferred_element_type=F32) * gate[here].reshape(rows * width, -1)
-        out_ref[here] = update.astype(BF16).reshape(rows, width, -1)
-
-    wide = 2 * rows
-    width = max(-(-(s * wide % 8 + wide) // 8) * 8 for s in range(span))
-    start = jnp.minimum(last * wide // 8 * 8, cols - width)
+    @pl.when(helped)
+    def _():
+        @pl.loop(0, pairs - once)
+        def _(d):
+            held = other.at[:, pl.ds(d * step, step)]
+            pltpu.make_async_remote_copy(
+                src_ref=held, dst_ref=held, send_sem=other_send, recv_sem=other_recv.at[d],
+                device_id={"row": row, "col": c}, device_id_type=MESH,
+            ).wait_recv()
+            sums(y, other, d, lambda i, j, value: place(i, j, last, once + d, 1 - y, value))
+
+    loads[4].wait()
     every = pl.ds(0, pairs)
-    some = pl.ds(0, once)
-
-    @pl.loop(0, twice)
-    def _(d):
-        @pl.when(d == twice - 1)
-        def _():
-            pl.loop(0, span - 1)(lambda t: collect(order(t) - low, every, pairs))
-            loads[4].wait()
-            if span == 2:
-                finish(jnp.where(start == 0, width, 0), cols - width)
-            else:
-                @pl.loop(0, cols // 8)
-                def _(b):
-                    @pl.when((8 * b < start) | (8 * b >= start + width))
-                    def _():
-                        finish(8 * b, 8)
-
-        @pl.when(helped)
-        def _():
-            other_copy(last, d, 1).wait_recv()
-            sums(y, other, d, lambda i, j, value: place(i, j, last, once + d, 1 - y, value))
-
-    pl.when(helped)(lambda: collect(last, some, once))
+    pl.loop(0, span - 1)(lambda t: collect(order(t) - low, every, pairs))
     pl.when(jnp.logical_not(helped))(lambda: collect(last, every, pairs))
-    finish(start, width)
+    for count in (twice, LESS):
+        some = pl.ds(0, pairs - count)
+        pl.when(helped & (once == pairs - count))(lambda some=some, count=count: collect(last, some, pairs - count))
+    @pl.when(row >= 0)
+    def _():
+        tri = layer_norm(comb[...].reshape(flat, hid)).astype(BF16)
+        update = jnp.dot(tri, wo_ref[...], preferred_element_type=F32) * gate[...].reshape(flat, -1)
+        out_ref[...] = update.astype(BF16).reshape(rows, cols, -1)
+
     @pl.loop(0, span)
     def _(slot):
         kept = far & (y == 1) & (slot == last)
-        pl.when(kept)(lambda: ret_copy(stage.at[slot, some], back.at[slot, some], slot).wait_send())
         pl.when(jnp.logical_not(kept))(lambda: ret_copy(stage.at[slot], back.at[slot], slot).wait_send())
+        for count in (twice, LESS):
+            some = pl.ds(0, pairs - count)
+
+            @pl.when(kept & (once == pairs - count))
+            def _(some=some):
+                ret_copy(stage.at[slot, some], back.at[slot, some], slot).wait_send()
 
 
 def per_device(n, pair_rep, proj_weight, gate_weight, out_weight):
@@ -323,7 +346,7 @@
     hid = out_weight.shape[0]
     flat = rows * cols
     pairs = rows // 2
-    twice = pairs // 2
+    twice = TWICE
     span = n // 4
     padded = -(-2 * rows // 8) * 8
     vmem = pl.BlockSpec(memory_space=pltpu.VMEM)
@@ -342,7 +365,7 @@
             dma((5,)),
             pltpu.VMEM((flat, hid), BF16),
             pltpu.VMEM((span, 2, flat, hid), BF16),
-            pltpu.VMEM((2, 2, flat, hid), BF16),
+            pltpu.VMEM((4, flat, hid), BF16),
             pltpu.VMEM((2, 2, flat, hid), F32),
             pltpu.VMEM((rows, cols, hid), F32),
             pltpu.VMEM((rows, cols, channels), F32),
@@ -352,7 +375,7 @@
             dma((4,)),
             dma((span,)),
             dma((span, pairs)),
-            dma((3,)),
+            dma,
             dma((2,)),
             dma((span,)),
             dma((span,)),

time: 15.3 us -> 15.2 us (level)
  no operation moved by 1% of the time
where the time goes in v3:
time: 15.2 us; the launch traced here: 15 us
  Pallas kernels  14.4 us (95%)
  local copies, waits for them, and re-layouts  0.64 us (4%)
    pallas_call x1, Pallas kernels, per_device(): pl.pallas_call(functools.partial(kernel, n, rows, cols, pairs, twice), ou...  14.4 us
    unnamed x1, local copies, waits for them, and re-layouts  0.64 us

profile of v3, /device:TPU:1, one launch (start us, length us, event | category | flops | bytes accessed | tf_op | source)
XLA Modules:
  0.0 15.0 jit_solution(10062570423999586336)
XLA Ops:
  0.0 14.4 %shard_map.46 = bf16[10,40,128]{2,1,0:T(8,128)(2,1)S(1)} custom-call(bf16[400,128]{1,0:T(8,128)(2,1)} %bitcast.1, bf16[128,512]{1,0:T(8,128)(2,1)} %wp_hbm.1, bf16[128,128]{1,0:T(8,128)(2,1)} %wg_hbm.1, bf16[128,128]{1,0:T(8,128)(2,1)} %wo_hbm.1), custom_call_target="tpu_custom_call" | custom-call | tf_op jit(solution)/shard_map/pallas_call | solution.py:354
  14.4 0.6 %copy.6 = bf16[10,40,128]{2,1,0:T(8,128)(2,1)} copy(bf16[10,40,128]{2,1,0:T(8,128)(2,1)S(1)} %shard_map.46) | data formatting | bytes 204800

commit v4 on v3

--- a/solution.py
+++ b/solution.py
@@ -23,10 +23,11 @@
 
 def kernel(
     n, rows, cols, pairs, twice, x_hbm, wp_hbm, wg_hbm, wo_hbm, out_ref,
-    x_ref, wp_ref, wg_ref, wo_ref, normed, in_sem, own, right, left, left32, comb, gate, stage, back, other,
+    x_ref, wp_ref, w_ref, normed, in_sem, own, right, left, left32, comb, gate, stage, back, other,
     own_send, fwd_send, recv, lsend, lrecv, ret_send, ret_recv, other_send, other_recv,
 ):
-    hid = wo_ref.shape[0]
+    hid, channels = wo_hbm.shape
+    wg_ref, wo_ref = w_ref.at[pl.ds(0, channels)], w_ref.at[pl.ds(channels, hid)]
     flat = rows * cols
     step = flat // pairs
     loads = [pltpu.make_async_copy(x_hbm, x_ref, in_sem.at[0])]
@@ -34,7 +35,7 @@
         cut = (slice(None), pl.ds(2 * hid * k, 2 * hid))
         loads.append(pltpu.make_async_copy(wp_hbm.at[cut], wp_ref.at[k], in_sem.at[len(loads)]))
     loads.append(pltpu.make_async_copy(wg_hbm, wg_ref, in_sem.at[3]))
-    loads.append(pltpu.make_async_copy(wo_hbm, wo_ref, in_sem.at[4]))
+    loads.append(pltpu.make_async_copy(wo_hbm, wo_ref, in_sem.at[3]))
     for load in loads:
         load.start()
     deep = n // 2
@@ -140,7 +141,7 @@
     to_across.start()
     to_sibling.start()
     left32[y, c] = left[2 * c + y].astype(F32)
-    loads[3].wait()
+    pltpu.make_async_copy(w_ref, w_ref, in_sem.at[3]).wait()
     opened = jax.nn.sigmoid(jnp.dot(normed[...], wg_ref[...], preferred_element_type=F32))
     gate[...] = opened.reshape(rows, cols, -1)
 
@@ -237,7 +238,7 @@
 
     last = order(span - 1) - low
 
-    lead = pairs // 2
+    lead = 1
 
     def combine(index):
         zs = order(index // pairs)
@@ -316,7 +317,6 @@
             ).wait_recv()
             sums(y, other, d, lambda i, j, value: place(i, j, last, once + d, 1 - y, value))
 
-    loads[4].wait()
     every = pl.ds(0, pairs)
     pl.loop(0, span - 1)(lambda t: collect(order(t) - low, every, pairs))
     pl.when(jnp.logical_not(helped))(lambda: collect(last, every, pairs))
@@ -359,10 +359,9 @@
         scratch_shapes=[
             pltpu.VMEM((flat, channels), BF16),
             pltpu.VMEM((2, channels, 2 * hid), BF16),
-            pltpu.VMEM((channels, channels), BF16),
-            pltpu.VMEM((hid, channels), BF16),
+            pltpu.VMEM((channels + hid, channels), BF16),
             pltpu.VMEM((flat, channels), BF16),
-            dma((5,)),
+            dma((4,)),
             pltpu.VMEM((flat, hid), BF16),
             pltpu.VMEM((span, 2, flat, hid), BF16),
             pltpu.VMEM((4, flat, hid), BF16),

time: 15.2 us -> 15.2 us (level)
  no operation moved by 1% of the time
where the time goes in v4:
time: 15.2 us; the launch traced here: 15 us
  Pallas kernels  14.4 us (95%)
  local copies, waits for them, and re-layouts  0.64 us (4%)
    pallas_call x1, Pallas kernels, per_device(): pl.pallas_call(functools.partial(kernel, n, rows, cols, pairs, twice), ou...  14.4 us
    unnamed x1, local copies, waits for them, and re-layouts  0.64 us

profile of v4, /device:TPU:1, one launch (start us, length us, event | category | flops | bytes accessed | tf_op | source)
XLA Modules:
  0.0 15.0 jit_solution(12634996323560192351)
XLA Ops:
  0.0 14.4 %shard_map.46 = bf16[10,40,128]{2,1,0:T(8,128)(2,1)S(1)} custom-call(bf16[400,128]{1,0:T(8,128)(2,1)} %bitcast.1, bf16[128,512]{1,0:T(8,128)(2,1)} %wp_hbm.1, bf16[128,128]{1,0:T(8,128)(2,1)} %wg_hbm.1, bf16[128,128]{1,0:T(8,128)(2,1)} %wo_hbm.1), custom_call_target="tpu_custom_call" | custom-call | tf_op jit(solution)/shard_map/pallas_call | solution.py:354
  14.4 0.6 %copy.6 = bf16[10,40,128]{2,1,0:T(8,128)(2,1)} copy(bf16[10,40,128]{2,1,0:T(8,128)(2,1)S(1)} %shard_map.46) | data formatting | bytes 204800

commit v5 on v4

--- a/solution.py
+++ b/solution.py
@@ -154,7 +154,7 @@
 
     def block(part, slot, q, r):
         return pltpu.make_async_remote_copy(
-            src_ref=part, dst_ref=part, send_sem=fwd_send.at[slot],
+            src_ref=part, dst_ref=part, send_sem=fwd_send,
             recv_sem=recv.at[slot, q], device_id={"row": r, "col": c}, device_id_type=MESH,
         )
 
@@ -285,11 +285,11 @@
         device_id={"row": row, "col": 1 - c}, device_id_type=MESH,
     ).wait_send()
 
-    @pl.loop(0, span)
-    def _(slot):
-        @pl.when(passes(slot + low))
-        def _():
-            block(right.at[slot], slot, 0, row).wait_send()
+    passing = sum(passes(s + low).astype(jnp.int32) for s in range(span))
+    for count in range(1, span + 1):
+        @pl.when(passing == count)
+        def _(count=count):
+            block(right.at[pl.ds(0, count)], 0, 0, row).wait_send()
 
     for count in (twice, LESS):
         @pl.when(helps & (once_there == pairs - count))
@@ -372,7 +372,7 @@
             pltpu.VMEM((span, pairs, padded, hid), F32),
             pltpu.VMEM((2, twice * (flat // pairs), hid), BF16),
             dma((4,)),
-            dma((span,)),
+            dma,
             dma((span, pairs)),
             dma,
             dma((2,)),

time: 15.2 us -> 15.2 us (level)
  no operation moved by 1% of the time
where the time goes in v5:
time: 15.2 us; the launch traced here: 15 us
  Pallas kernels  14.4 us (95%)
  local copies, waits for them, and re-layouts  0.64 us (4%)
    pallas_call x1, Pallas kernels, per_device(): pl.pallas_call(functools.partial(kernel, n, rows, cols, pairs, twice), ou...  14.4 us
    unnamed x1, local copies, waits for them, and re-layouts  0.64 us

profile of v5, /device:TPU:1, one launch (start us, length us, event | category | flops | bytes accessed | tf_op | source)
XLA Modules:
  0.0 15.0 jit_solution(6540412544955420974)
XLA Ops:
  0.0 14.4 %shard_map.46 = bf16[10,40,128]{2,1,0:T(8,128)(2,1)S(1)} custom-call(bf16[400,128]{1,0:T(8,128)(2,1)} %bitcast.1, bf16[128,512]{1,0:T(8,128)(2,1)} %wp_hbm.1, bf16[128,128]{1,0:T(8,128)(2,1)} %wg_hbm.1, bf16[128,128]{1,0:T(8,128)(2,1)} %wo_hbm.1), custom_call_target="tpu_custom_call" | custom-call | tf_op jit(solution)/shard_map/pallas_call | solution.py:354
  14.4 0.6 %copy.6 = bf16[10,40,128]{2,1,0:T(8,128)(2,1)} copy(bf16[10,40,128]{2,1,0:T(8,128)(2,1)S(1)} %shard_map.46) | data formatting | bytes 204800
